TPU v7x, 32 devices: a whole 2x2x4 slice. The times are simulated.
32 devices in a mesh: size: 4 (over z), gz: 8 (over y, x, core).
Axes of the slice: x: 2, y: 2, z: 4, core: 2. Of those that a mesh axis runs over, the one named last changes fastest.
Arguments:
- tissue: int32 [256, 64, 128], P('gz'), may hold values from 0 to 2
- vessel_pressure: float32 [256, 64, 128], P('gz', 'size'), may hold values from -12 to 12
- cond_table: float32 [3], replicated, may hold values from 0.4 to 1.2
- leak_table: float32 [3], replicated, may hold values from 0.2 to 2
- bind_table: float32 [4, 3], P('size'), may hold values from 0.05 to 1
- hindrance: float32 [4], P('size'), may hold values from 0.2 to 1
- diffusivity: float32 [4], P('size'), may hold values from 0.1 to 0.6
- free_conc: float32 [4, 256, 64, 128], P('size', 'gz'), may hold values from 0 to 2
- bound_conc: float32 [4, 256, 64, 128], P('size', 'gz'), may hold values from 0 to 1
Outputs:
- pressure: float32 [256, 64, 128], P('gz', 'size')
- free_out: float32 [4, 256, 64, 128], P('size', 'gz')
- bound_out: float32 [4, 256, 64, 128], P('size', 'gz')
Inputs may be any that keep to these rules, and one draw needn't show every extreme that they name: 0 marks a vessel cell, 1 necrotic tissue, 2 viable tissue.
All inputs are finite; a program needn't handle non-finite values.
Results may differ from a plain program's by a relative error of at most 0.0001.
Values sent between devices are 32-bit elements; how exact they have to be, the bound alone decides.
No kernel may reach another device: no remote copies, remote signals or barrier semaphores. Data moves between devices by JAX's collectives and lax.ppermute only.
A program may use at most 128 MiB of HBM per device.

v0:
```python
import jax
import jax.numpy as jnp
from jax import lax
from jax.sharding import PartitionSpec as P

ITERS = 2
TSTEPS = 2
time_step = 0.1


def extended(cells, sides, width):
    for axis, dim in sides:
        count = lax.axis_size(axis)
        ends = count - 1
        head = lax.slice_in_dim(cells, 0, width, axis=dim)
        tail = lax.slice_in_dim(cells, cells.shape[dim] - width, cells.shape[dim], axis=dim)
        cells = jnp.concatenate(
            [
                lax.ppermute(tail, axis, [(i, (i + 1) % count) for i in range(ends)]),
                cells,
                lax.ppermute(head, axis, [((i + 1) % count, i) for i in range(ends)]),
            ],
            axis=dim,
        )
    return cells


def lookup(table, labels):
    return jnp.where(labels == 0, table[0], jnp.where(labels == 1, table[1], table[2]))


def neighbours(padded):
    total = padded[2:, 1:-1, 1:-1] + padded[:-2, 1:-1, 1:-1]
    total = total + padded[1:-1, 2:, 1:-1] + padded[1:-1, :-2, 1:-1]
    total = total + padded[1:-1, 1:-1, 2:] + padded[1:-1, 1:-1, :-2]
    return total


def apply_operator(vector, conduct, leak):
    scaled = conduct * vector
    rimmed = extended(scaled, (("size", 1), ("gz", 0)), 1)
    padded = jnp.pad(rimmed, ((0, 0), (0, 0), (1, 1)))
    return conduct * (6.0 * scaled - neighbours(padded)) + leak * vector


def paired_products(residual, precond, image):
    return lax.psum((jnp.sum(residual * precond), jnp.sum(precond * image)), ("size", "gz"))


def along_line(array, along_dim):
    return array[tuple((slice(None) if k == along_dim else slice(1, -1) for k in range(3)))]


def lower_part(array, along_dim):
    return array[tuple((slice(0, -1) if k == along_dim else slice(None) for k in range(3)))]


def upper_part(array, along_dim):
    return array[tuple((slice(1, None) if k == along_dim else slice(None) for k in range(3)))]


def transport_step(conc_pad, fields_pad, hinder, diffuse):
    divergence = None
    for along_dim in range(3):
        conc_line = along_line(conc_pad, along_dim)
        press_line = along_line(fields_pad[0], along_dim)
        cond_line = along_line(fields_pad[1], along_dim)
        conc_low = lower_part(conc_line, along_dim)
        conc_high = upper_part(conc_line, along_dim)
        velocity = (
            hinder
            * lower_part(cond_line, along_dim)
            * upper_part(cond_line, along_dim)
            * (lower_part(press_line, along_dim) - upper_part(press_line, along_dim))
        )
        flux = (
            jnp.maximum(velocity, 0.0) * conc_low
            + jnp.minimum(velocity, 0.0) * conc_high
            + diffuse * (conc_low - conc_high)
        )
        term = upper_part(flux, along_dim) - lower_part(flux, along_dim)
        divergence = term if divergence is None else divergence + term
    conc = conc_pad[1:-1, 1:-1, 1:-1]
    rate = fields_pad[2][1:-1, 1:-1, 1:-1]
    bind = rate * conc
    return (conc - time_step * (divergence + bind), bind)


def pad_plane(array):
    return jnp.pad(array, ((0, 0), (1, 1), (1, 1)))


def local(
    tissue,
    vessel_pressure,
    cond_table,
    leak_table,
    bind_table,
    hindrance,
    diffusivity,
    free_conc,
    bound_conc,
):
    block_x = vessel_pressure.shape[1]
    slab_z = vessel_pressure.shape[0]
    local_tissue = lax.dynamic_slice_in_dim(tissue, lax.axis_index("size") * block_x, block_x, 1)
    conduct = lookup(cond_table, local_tissue)
    leak = lookup(leak_table, local_tissue)
    diag = 6.0 * conduct * conduct + leak
    source = leak * vessel_pressure
    solution = jnp.zeros_like(source)
    residual = source
    precond = residual / diag
    image = apply_operator(precond, conduct, leak)
    rho_now, product = paired_products(residual, precond, image)
    alpha = rho_now / product
    direction = precond
    along_image = image
    for iteration in range(ITERS):
        solution = solution + alpha * direction
        residual = residual - alpha * along_image
        if iteration + 1 < ITERS:
            precond = residual / diag
            image = apply_operator(precond, conduct, leak)
            rho_next, product = paired_products(residual, precond, image)
            ratio = rho_next / rho_now
            alpha = rho_next / (product - ratio * rho_next / alpha)
            direction = precond + ratio * direction
            along_image = image + ratio * along_image
            rho_now = rho_next
    conduct_slab = lookup(cond_table, tissue)
    rate_slab = lookup(bind_table[0], tissue)
    slab_pressure = lax.all_gather(solution, "size", axis=1, tiled=True)
    stacked = jnp.stack([slab_pressure, conduct_slab, rate_slab])
    rimmed = extended(stacked, (("gz", 1),), TSTEPS)
    fields_pad = jnp.pad(rimmed, ((0, 0), (0, 0), (1, 1), (1, 1)))
    hinder = hindrance[0]
    diffuse = diffusivity[0]
    conc = free_conc[0]
    bound = bound_conc[0]
    fields_one = fields_pad[:, TSTEPS - 1 : TSTEPS + 1 + slab_z]
    for sweep in range(TSTEPS):
        conc_pad = pad_plane(extended(conc, (("gz", 0),), 1))
        conc, bind = transport_step(conc_pad, fields_one, hinder, diffuse)
        bound = bound + time_step * bind
    return (solution, conc[None], bound[None])


def solution(mesh):
    return jax.shard_map(
        local,
        mesh=mesh,
        in_specs=(
            P("gz", None, None),
            P("gz", "size", None),
            P(),
            P(),
            P("size", None),
            P("size"),
            P("size"),
            P("size", "gz", None, None),
            P("size", "gz", None, None),
        ),
        out_specs=(P("gz", "size", None), P("size", "gz", None, None), P("size", "gz", None, None)),
        check_vma=False,
    )
```

profile of v0, /device:TPU:4, one launch (start us, length us, event | category | flops | bytes accessed | tf_op | source)
XLA Modules:
  0.0 228.2 jit_solution(11120340233154857061)
XLA Ops:
  10.0 4.9 %fusion.39 = (f32[32,16,128]{2,1,0:T(8,128)S(1)}, pred[32,16,128]{2,1,0:T(8,128)(4,1)S(1)}, pred[32,16,128]{2,1,0:T(8,128)(4,1)S(1)}) fusion(f32[]{:T(128)} %bitcast.5, f32[]{:T(128)} %bitcast.4, f32[]{:T(128)} %bitcast.3, f32[32,16,128]{2,1,0:T(8,128)} %param.10, f32[]{:T(128)} %bitcast.2, f32[]{:T(128)} %bitcast.1, f32[]{:T(128)} %bitcast, ...), kind=kLoop, calls=%fused_computation.127 | loop fusion | flops 786432 | bytes 917532 | tf_op jit(solution)/shard_map/mul | solution.py:40
  16.3 4.5 %collective-permute-start = (f32[32,1,128]{2,1,0:T(1,128)S(1)}, f32[32,1,128]{2,1,0:T(1,128)S(1)}, u32[]{:S(2)}, u32[]{:S(2)}) collective-permute-start(f32[32,1,128]{2,1,0:T(1,128)S(1)} %get-tuple-element.41), channel_id=1, source_target_pairs={{0,8},{8,16},{16,24},{1,9},{9,17},{17,25},{2,10},{10,18},{18,26},{... | collective-permute-start | bytes 49160 | tf_op jit(solution)/shard_map/ppermute | solution.py:19
  24.2 2.4 %collective-permute-start.3 = (f32[1,18,128]{2,1,0:T(8,128)S(1)}, f32[1,18,128]{2,1,0:T(8,128)S(1)}, u32[]{:S(2)}, u32[]{:S(2)}) collective-permute-start(f32[1,18,128]{2,1,0:T(8,128)S(1)} %get-tuple-element.37), channel_id=1, source_target_pairs={{0,1},{1,2},{2,3},{3,4},{4,5},{5,6},{6,7},{8,9},{9,10},{10,11},{11... | collective-permute-start | bytes 27656 | tf_op jit(solution)/shard_map/ppermute | solution.py:19
  26.6 3.5 %collective-permute-done.3 = f32[1,18,128]{2,1,0:T(8,128)S(1)} collective-permute-done((f32[1,18,128]{2,1,0:T(8,128)S(1)}, f32[1,18,128]{2,1,0:T(8,128)S(1)}, u32[]{:S(2)}, u32[]{:S(2)}) %collective-permute-start.3) | collective-permute-done | bytes 9248 | tf_op jit(solution)/shard_map/ppermute | solution.py:19
  30.5 4.7 %multiply_reduce_fusion.1 = (f32[]{:T(128)}, f32[]{:T(128)}, f32[32,16,128]{2,1,0:T(8,128)S(1)}) fusion(pred[32,16,128]{2,1,0:T(8,128)(4,1)S(1)} %get-tuple-element.23, pred[32,16,128]{2,1,0:T(8,128)(4,1)S(1)} %get-tuple-element.22, f32[]{:T(128)} %bitcast.5, f32[]{:T(128)} %bitcast.4, f32[]{:T(128)} %bitcast.3, f32[32,16,128]{2,1,0:T(8,128)S(1)} %copy-done.1, ...), kind=kLoop, calls=%fused_computation.123 | loop fusion | flops 2031614 | bytes 1493024 | tf_op jit(solution)/shard_map/reduce_sum | solution.py:47
  35.3 41.6 %all-reduce.6 = (f32[]{:T(128)}, f32[]{:T(128)}) all-reduce(f32[]{:T(128)} %get-tuple-element.4, f32[]{:T(128)} %get-tuple-element.3), channel_id=1, replica_groups=mesh['size'=4,'gz'=8] {'size','gz'}, use_global_device_ids=true, to_apply=%region_1.2 | all-reduce | flops 2 | bytes 16 | tf_op jit(solution)/shard_map/psum | solution.py:47
  78.1 4.5 %fusion.38 = (f32[32,16,128]{2,1,0:T(8,128)S(1)}, f32[]{:T(128)}) fusion(pred[32,16,128]{2,1,0:T(8,128)(4,1)S(1)} %get-tuple-element.23, pred[32,16,128]{2,1,0:T(8,128)(4,1)S(1)} %get-tuple-element.22, f32[]{:T(128)} %bitcast.5, f32[]{:T(128)} %bitcast.4, f32[]{:T(128)} %bitcast.3, f32[32,16,128]{2,1,0:T(8,128)S(1)} %get-tuple-element.20, f32[]{:T(128)S(6)} %div.19, ...), kind=kLoop, calls=%fused_computation.126 | loop fusion | flops 917503 | bytes 917536 | tf_op jit(solution)/shard_map/mul | solution.py:40
  84.2 4.7 %collective-permute-start.4 = (f32[32,1,128]{2,1,0:T(1,128)S(1)}, f32[32,1,128]{2,1,0:T(1,128)S(1)}, u32[]{:S(2)}, u32[]{:S(2)}) collective-permute-start(f32[32,1,128]{2,1,0:T(1,128)S(1)} %get-tuple-element.39), channel_id=1, source_target_pairs={{0,8},{8,16},{16,24},{1,9},{9,17},{17,25},{2,10},{10,18},{18,26},{... | collective-permute-start | bytes 49160 | tf_op jit(solution)/shard_map/ppermute | solution.py:19
  92.2 2.4 %collective-permute-start.7 = (f32[1,18,128]{2,1,0:T(8,128)S(1)}, f32[1,18,128]{2,1,0:T(8,128)S(1)}, u32[]{:S(2)}, u32[]{:S(2)}) collective-permute-start(f32[1,18,128]{2,1,0:T(8,128)S(1)} %get-tuple-element.35), channel_id=1, source_target_pairs={{0,1},{1,2},{2,3},{3,4},{4,5},{5,6},{6,7},{8,9},{9,10},{10,11},{11... | collective-permute-start | bytes 27656 | tf_op jit(solution)/shard_map/ppermute | solution.py:19
  94.6 3.5 %collective-permute-done.7 = f32[1,18,128]{2,1,0:T(8,128)S(1)} collective-permute-done((f32[1,18,128]{2,1,0:T(8,128)S(1)}, f32[1,18,128]{2,1,0:T(8,128)S(1)}, u32[]{:S(2)}, u32[]{:S(2)}) %collective-permute-start.7) | collective-permute-done | bytes 9248 | tf_op jit(solution)/shard_map/ppermute | solution.py:19
  98.5 4.8 %fusion.28 = f32[]{:T(128)} fusion(f32[34,18,130]{2,1,0:T(8,128)S(1)} %select_maximum_fusion.8, f32[32,16,128]{2,1,0:T(8,128)S(1)} %get-tuple-element.33, f32[32,1,128]{2,1,0:T(1,128)S(1)} %collective-permute-done.4, f32[32,1,128]{2,1,0:T(1,128)S(1)} %collective-permute-done.5, f32[1,18,128]{2,1,0:T(8,128)S(1)} %collective-permute-done.7, ...), kind=kLoop, calls=%fused_computation.91 | loop fusion | flops 2031615 | bytes 1493024 | tf_op jit(solution)/shard_map/reduce_sum | solution.py:47
  103.3 41.4 %all-reduce.5 = (f32[]{:T(128)}, f32[]{:T(128)}) all-reduce(f32[]{:T(128)} %get-tuple-element.34, f32[]{:T(128)} %fusion.28), channel_id=1, replica_groups=mesh['size'=4,'gz'=8] {'size','gz'}, use_global_device_ids=true, to_apply=%region_5.6 | all-reduce | flops 2 | bytes 16 | tf_op jit(solution)/shard_map/psum | solution.py:47
  149.1 4.6 %multiply_add_fusion.6 = f32[32,16,128]{2,1,0:T(8,128)} fusion(f32[]{:T(128)S(6)} %div.21, f32[]{:T(128)S(6)} %div.23, f32[]{:T(128)S(6)} %div.19, pred[32,16,128]{2,1,0:T(8,128)(4,1)S(1)} %get-tuple-element.23, pred[32,16,128]{2,1,0:T(8,128)(4,1)S(1)} %get-tuple-element.22, f32[]{:T(128)} %bitcast.5, f32[]{:T(128)} %bitcast.4, f32[]{:T(128)} %bitcast.3, ...), kind=kLoop, calls=%fused_computation.120 | loop fusion | flops 1114112 | bytes 917540 | tf_op jit(solution)/shard_map/add | solution.py:120
  155.7 2.3 %collective-permute-start.10 = (f32[1,64,128]{2,1,0:T(8,128)S(1)}, f32[1,64,128]{2,1,0:T(8,128)S(1)}, u32[]{:S(2)}, u32[]{:S(2)}) collective-permute-start(f32[1,64,128]{2,1,0:T(8,128)S(1)} %get-tuple-element.31), channel_id=1, source_target_pairs={{0,1},{1,2},{2,3},{3,4},{4,5},{5,6},{6,7},{8,9},{9,10},{10,11},{11... | collective-permute-start | bytes 98312 | tf_op jit(solution)/shard_map/ppermute | solution.py:19
  160.0 2.2 select_bitcast_fusion.1
  164.3 17.5 %all-gather.2.cloned.1.call-done = f32[32,64,128]{2,1,0:T(8,128)} async-done(((f32[32,16,128]{2,1,0:T(8,128)}), f32[32,64,128]{2,1,0:T(8,128)}) %all-gather.2.cloned.1.call-update) | async-done | bytes 1048592 | tf_op jit(solution)/shard_map/all_gather | solution.py:133
  182.7 2.4 %collective-permute-start.9 = (f32[3,2,64,128]{3,2,1,0:T(8,128)S(1)}, f32[3,2,64,128]{3,2,1,0:T(8,128)S(1)}, u32[]{:S(2)}, u32[]{:S(2)}) collective-permute-start(f32[3,2,64,128]{3,2,1,0:T(8,128)S(1)} %get-tuple-element.28), channel_id=1, source_target_pairs={{1,0},{2,1},{3,2},{4,3},{5,4},{6,5},{7,6},{9,8},{10,9},{11,10},{12... | collective-permute-start | bytes 589832 | tf_op jit(solution)/shard_map/ppermute | solution.py:21
  185.1 2.2 collective-permute-start.8
  188.2 4.7 %collective-permute-done.8 = f32[3,2,64,128]{3,2,1,0:T(8,128)S(1)} collective-permute-done((f32[3,2,64,128]{3,2,1,0:T(8,128)S(1)}, f32[3,2,64,128]{3,2,1,0:T(8,128)S(1)}, u32[]{:S(2)}, u32[]{:S(2)}) %collective-permute-start.8) | collective-permute-done | bytes 196640 | tf_op jit(solution)/shard_map/ppermute | solution.py:19
  193.0 7.3 %select_maximum_fusion = f32[3,36,66,130]{3,2,1,0:T(8,128)S(1)} fusion(f32[3,2,64,128]{3,2,1,0:T(8,128)S(1)} %collective-permute-done.9, f32[3,2,64,128]{3,2,1,0:T(8,128)S(1)} %collective-permute-done.8, f32[1,32,64,128]{3,2,1,0:T(8,128)S(1)} %select_bitcast_fusion, f32[1,32,64,128]{3,2,1,0:T(8,128)S(1)} %get-tuple-element.17, f32[1,32,64,128]{3,2,1,0:T(8,128)S(1)} %bitcast.52), kind=kLoop, calls=%fused_computation.4 | loop fusion | flops 19459440 | bytes 7245504 | tf_op jit(solution)/shard_map/concatenate | solution.py:17
  200.9 2.4 %multiply_add_fusion.1 = (f32[32,64,129]{2,1,0:T(8,128)S(1)}, f32[32,64,129]{2,1,0:T(8,128)S(1)}) fusion(f32[34,66,130]{2,1,0:T(8,128)S(1)} %select_maximum_fusion.6, f32[]{:T(128)} %bitcast.45, f32[34,66,130]{2,1,0:T(8,128)S(1)} %get-tuple-element.25, f32[34,66,130]{2,1,0:T(8,128)S(1)} %get-tuple-element.24, f32[]{:T(128)} %bitcast.42), kind=kLoop, calls=%fused_computation.30 | loop fusion | flops 3170304 | bytes 8454152 | tf_op jit(solution)/shard_map/add | solution.py:77
  206.5 2.1 fusion.21
  210.4 2.6 %collective-permute-start.12 = (f32[1,64,128]{2,1,0:T(8,128)S(1)}, f32[1,64,128]{2,1,0:T(8,128)S(1)}, u32[]{:S(2)}, u32[]{:S(2)}) collective-permute-start(f32[1,64,128]{2,1,0:T(8,128)S(1)} %get-tuple-element.29), channel_id=1, source_target_pairs={{0,1},{1,2},{2,3},{3,4},{4,5},{5,6},{6,7},{8,9},{9,10},{10,11},{11... | collective-permute-start | bytes 98312 | tf_op jit(solution)/shard_map/ppermute | solution.py:19
  213.1 3.5 %collective-permute-done.12 = f32[1,64,128]{2,1,0:T(8,128)S(1)} collective-permute-done((f32[1,64,128]{2,1,0:T(8,128)S(1)}, f32[1,64,128]{2,1,0:T(8,128)S(1)}, u32[]{:S(2)}, u32[]{:S(2)}) %collective-permute-start.12) | collective-permute-done | bytes 32800 | tf_op jit(solution)/shard_map/ppermute | solution.py:19
  (60 shorter events, 30.1 us)
Async XLA Ops:
  7.2 23.3 %copy-start.1 = (f32[32,16,128]{2,1,0:T(8,128)S(1)}, f32[32,16,128]{2,1,0:T(8,128)}, u32[]{:S(2)}) copy-start(f32[32,16,128]{2,1,0:T(8,128)} %param.10) | copy-start | bytes 786436
  7.2 174.6 %all-gather.2.cloned.1.call-start = ((), (), s32[]{:S(2)}) async-start(), calls=%async_computation | async-start | bytes 1310720 | tf_op jit(solution)/shard_map/all_gather | solution.py:133
  15.0 5.9 %collective-permute-start.1 = (f32[32,1,128]{2,1,0:T(1,128)S(1)}, f32[32,1,128]{2,1,0:T(1,128)S(1)}, u32[]{:S(2)}, u32[]{:S(2)}) collective-permute-start(f32[32,1,128]{2,1,0:T(1,128)S(1)} %get-tuple-element.42), channel_id=1, source_target_pairs={{8,0},{16,8},{24,16},{9,1},{17,9},{25,17},{10,2},{18,10},{26,18},{... | collective-permute-start | bytes 49160 | tf_op jit(solution)/shard_map/ppermute | solution.py:21
  16.3 6.0 %collective-permute-start = (f32[32,1,128]{2,1,0:T(1,128)S(1)}, f32[32,1,128]{2,1,0:T(1,128)S(1)}, u32[]{:S(2)}, u32[]{:S(2)}) collective-permute-start(f32[32,1,128]{2,1,0:T(1,128)S(1)} %get-tuple-element.41), channel_id=1, source_target_pairs={{0,8},{8,16},{16,24},{1,9},{9,17},{17,25},{2,10},{10,18},{18,26},{... | collective-permute-start | bytes 49160 | tf_op jit(solution)/shard_map/ppermute | solution.py:19
  22.2 4.3 %collective-permute-start.2 = (f32[1,18,128]{2,1,0:T(8,128)S(1)}, f32[1,18,128]{2,1,0:T(8,128)S(1)}, u32[]{:S(2)}, u32[]{:S(2)}) collective-permute-start(f32[1,18,128]{2,1,0:T(8,128)S(1)} %get-tuple-element.38), channel_id=1, source_target_pairs={{1,0},{2,1},{3,2},{4,3},{5,4},{6,5},{7,6},{9,8},{10,9},{11,10},{12... | collective-permute-start | bytes 27656 | tf_op jit(solution)/shard_map/ppermute | solution.py:21
  24.2 5.9 %collective-permute-start.3 = (f32[1,18,128]{2,1,0:T(8,128)S(1)}, f32[1,18,128]{2,1,0:T(8,128)S(1)}, u32[]{:S(2)}, u32[]{:S(2)}) collective-permute-start(f32[1,18,128]{2,1,0:T(8,128)S(1)} %get-tuple-element.37), channel_id=1, source_target_pairs={{0,1},{1,2},{2,3},{3,4},{4,5},{5,6},{6,7},{8,9},{9,10},{10,11},{11... | collective-permute-start | bytes 27656 | tf_op jit(solution)/shard_map/ppermute | solution.py:19
  82.7 71.0 %copy-start = (f32[1,32,64,128]{3,2,1,0:T(8,128)S(1)}, f32[1,32,64,128]{3,2,1,0:T(8,128)}, u32[]{:S(2)}) copy-start(f32[1,32,64,128]{3,2,1,0:T(8,128)} %param.16) | copy-start | bytes 3145732
  82.7 6.1 %collective-permute-start.5 = (f32[32,1,128]{2,1,0:T(1,128)S(1)}, f32[32,1,128]{2,1,0:T(1,128)S(1)}, u32[]{:S(2)}, u32[]{:S(2)}) collective-permute-start(f32[32,1,128]{2,1,0:T(1,128)S(1)} %get-tuple-element.40), channel_id=1, source_target_pairs={{8,0},{16,8},{24,16},{9,1},{17,9},{25,17},{10,2},{18,10},{26,18},{... | collective-permute-start | bytes 49160 | tf_op jit(solution)/shard_map/ppermute | solution.py:21
  84.1 75.2 %copy-start.9 = (f32[1,3]{1,0:T(1,128)S(1)}, f32[1,3]{1,0:T(1,128)}, u32[]{:S(2)}) copy-start(f32[1,3]{1,0:T(1,128)} %param.13) | copy-start | bytes 40
  84.1 75.9 %copy-start.3 = (s32[32,64,128]{2,1,0:T(8,128)S(1)}, s32[32,64,128]{2,1,0:T(8,128)}, u32[]{:S(2)}) copy-start(s32[32,64,128]{2,1,0:T(8,128)} %param.9) | copy-start | bytes 3145732
  84.2 6.1 %collective-permute-start.4 = (f32[32,1,128]{2,1,0:T(1,128)S(1)}, f32[32,1,128]{2,1,0:T(1,128)S(1)}, u32[]{:S(2)}, u32[]{:S(2)}) collective-permute-start(f32[32,1,128]{2,1,0:T(1,128)S(1)} %get-tuple-element.39), channel_id=1, source_target_pairs={{0,8},{8,16},{16,24},{1,9},{9,17},{17,25},{2,10},{10,18},{18,26},{... | collective-permute-start | bytes 49160 | tf_op jit(solution)/shard_map/ppermute | solution.py:19
  90.3 4.3 %collective-permute-start.6 = (f32[1,18,128]{2,1,0:T(8,128)S(1)}, f32[1,18,128]{2,1,0:T(8,128)S(1)}, u32[]{:S(2)}, u32[]{:S(2)}) collective-permute-start(f32[1,18,128]{2,1,0:T(8,128)S(1)} %get-tuple-element.36), channel_id=1, source_target_pairs={{1,0},{2,1},{3,2},{4,3},{5,4},{6,5},{7,6},{9,8},{10,9},{11,10},{12... | collective-permute-start | bytes 27656 | tf_op jit(solution)/shard_map/ppermute | solution.py:21
  92.2 5.9 %collective-permute-start.7 = (f32[1,18,128]{2,1,0:T(8,128)S(1)}, f32[1,18,128]{2,1,0:T(8,128)S(1)}, u32[]{:S(2)}, u32[]{:S(2)}) collective-permute-start(f32[1,18,128]{2,1,0:T(8,128)S(1)} %get-tuple-element.35), channel_id=1, source_target_pairs={{0,1},{1,2},{2,3},{3,4},{4,5},{5,6},{6,7},{8,9},{9,10},{10,11},{11... | collective-permute-start | bytes 27656 | tf_op jit(solution)/shard_map/ppermute | solution.py:19
  153.7 33.6 %collective-permute-start.11 = (f32[1,64,128]{2,1,0:T(8,128)S(1)}, f32[1,64,128]{2,1,0:T(8,128)S(1)}, u32[]{:S(2)}, u32[]{:S(2)}) collective-permute-start(f32[1,64,128]{2,1,0:T(8,128)S(1)} %get-tuple-element.32), channel_id=1, source_target_pairs={{1,0},{2,1},{3,2},{4,3},{5,4},{6,5},{7,6},{9,8},{10,9},{11,10},{12... | collective-permute-start | bytes 98312 | tf_op jit(solution)/shard_map/ppermute | solution.py:21
  155.7 31.6 %collective-permute-start.10 = (f32[1,64,128]{2,1,0:T(8,128)S(1)}, f32[1,64,128]{2,1,0:T(8,128)S(1)}, u32[]{:S(2)}, u32[]{:S(2)}) collective-permute-start(f32[1,64,128]{2,1,0:T(8,128)S(1)} %get-tuple-element.31), channel_id=1, source_target_pairs={{0,1},{1,2},{2,3},{3,4},{4,5},{5,6},{6,7},{8,9},{9,10},{10,11},{11... | collective-permute-start | bytes 98312 | tf_op jit(solution)/shard_map/ppermute | solution.py:19
  182.6 10.3 %copy-start.2 = (f32[32,64,128]{2,1,0:T(8,128)S(1)}, f32[32,64,128]{2,1,0:T(8,128)}, u32[]{:S(2)}) copy-start(f32[32,64,128]{2,1,0:T(8,128)} %all-gather.2.cloned.1.call-done) | copy-start | bytes 3145732
  182.7 5.6 %collective-permute-start.9 = (f32[3,2,64,128]{3,2,1,0:T(8,128)S(1)}, f32[3,2,64,128]{3,2,1,0:T(8,128)S(1)}, u32[]{:S(2)}, u32[]{:S(2)}) collective-permute-start(f32[3,2,64,128]{3,2,1,0:T(8,128)S(1)} %get-tuple-element.28), channel_id=1, source_target_pairs={{1,0},{2,1},{3,2},{4,3},{5,4},{6,5},{7,6},{9,8},{10,9},{11,10},{12... | collective-permute-start | bytes 589832 | tf_op jit(solution)/shard_map/ppermute | solution.py:21
  185.1 7.9 %collective-permute-start.8 = (f32[3,2,64,128]{3,2,1,0:T(8,128)S(1)}, f32[3,2,64,128]{3,2,1,0:T(8,128)S(1)}, u32[]{:S(2)}, u32[]{:S(2)}) collective-permute-start(f32[3,2,64,128]{3,2,1,0:T(8,128)S(1)} %get-tuple-element.27), channel_id=1, source_target_pairs={{0,1},{1,2},{2,3},{3,4},{4,5},{5,6},{6,7},{8,9},{9,10},{10,11},{11... | collective-permute-start | bytes 589832 | tf_op jit(solution)/shard_map/ppermute | solution.py:19
  187.3 5.6 %copy-start.5 = (f32[1,64,128]{2,1,0:T(8,128)}, f32[1,64,128]{2,1,0:T(8,128)S(1)}, u32[]{:S(2)}) copy-start(f32[1,64,128]{2,1,0:T(8,128)S(1)} %collective-permute-done.11) | copy-start | bytes 98308
  187.3 5.6 %copy-start.7 = (f32[1,64,128]{2,1,0:T(8,128)}, f32[1,64,128]{2,1,0:T(8,128)S(1)}, u32[]{:S(2)}) copy-start(f32[1,64,128]{2,1,0:T(8,128)S(1)} %collective-permute-done.10) | copy-start | bytes 98308
  203.3 1.9 copy-start.6
  203.3 1.9 copy-start.8
  208.5 4.6 %collective-permute-start.13 = (f32[1,64,128]{2,1,0:T(8,128)S(1)}, f32[1,64,128]{2,1,0:T(8,128)S(1)}, u32[]{:S(2)}, u32[]{:S(2)}) collective-permute-start(f32[1,64,128]{2,1,0:T(8,128)S(1)} %get-tuple-element.30), channel_id=1, source_target_pairs={{1,0},{2,1},{3,2},{4,3},{5,4},{6,5},{7,6},{9,8},{10,9},{11,10},{12... | collective-permute-start | bytes 98312 | tf_op jit(solution)/shard_map/ppermute | solution.py:21
  210.4 6.1 %collective-permute-start.12 = (f32[1,64,128]{2,1,0:T(8,128)S(1)}, f32[1,64,128]{2,1,0:T(8,128)S(1)}, u32[]{:S(2)}, u32[]{:S(2)}) collective-permute-start(f32[1,64,128]{2,1,0:T(8,128)S(1)} %get-tuple-element.29), channel_id=1, source_target_pairs={{0,1},{1,2},{2,3},{3,4},{4,5},{5,6},{6,7},{8,9},{9,10},{10,11},{11... | collective-permute-start | bytes 98312 | tf_op jit(solution)/shard_map/ppermute | solution.py:19
  (1 other events, 1.2 us)
Sparse Core Ops, SparseCore 0:
  153.8 27.8 all-gather.1
where the time goes:
time: 229 us; the launch traced here: 228 us
  blocking collectives  83 us (36%)
  other arithmetic  49.8 us (22%)
  waiting for transfers between devices  35.7 us (16%)
  starting transfers between devices  34.1 us (15%)
  between operations  21.4 us (9%)
  local copies, waits for them, and re-layouts  4.21 us (2%)
    psum x2, blocking collectives, paired_products(): lax.psum((jnp.sum(residual * precond), jnp.sum(precond * image)), ('size'...  83 us
    ppermute x7, starting transfers between devices, extended(): lax.ppermute(tail, axis, [(i, (i + 1) % count) for i in range(ends)])  21.2 us
    ppermute x7, waiting for transfers between devices, extended(): lax.ppermute(tail, axis, [(i, (i + 1) % count) for i in range(ends)])  18 us
    all_gather x1, waiting for transfers between devices, local(): slab_pressure = lax.all_gather(solution, 'size', axis=1, tiled=True)  17.5 us
    ppermute x7, starting transfers between devices, extended(): lax.ppermute(head, axis, [((i + 1) % count, i) for i in range(ends)])  12.8 us
    concatenate x7, other arithmetic, extended(): jnp.concatenate([lax.ppermute(tail, axis, [(i, (i + 1) % count) for i in...  9.57 us
    reduce_sum x2, other arithmetic, paired_products(): jnp.sum(precond * image)  9.51 us
    mul x2, other arithmetic, apply_operator(): scaled = conduct * vector  9.43 us
  transfers between devices with their start and end apart: 15, of which 8 were waited for; matrix products, arithmetic and copies ran while one was open for 3% of the time, Pallas kernels for 0%

commit v1 on v0

--- a/solution.py
+++ b/solution.py
@@ -6,6 +6,11 @@
 ITERS = 2
 TSTEPS = 2
 time_step = 0.1
+
+
+def apply_weights(tile_in, a_name, along_axis="size"):
+    row_out = lax.psum(tile_in, axis_name=a_name)
+    return lax.psum(row_out, axis_name=along_axis)
 
 
 def extended(cells, sides, width):
@@ -44,7 +49,7 @@
 
 
 def paired_products(residual, precond, image):
-    return lax.psum((jnp.sum(residual * precond), jnp.sum(precond * image)), ("size", "gz"))
+    return apply_weights((jnp.sum(residual * precond), jnp.sum(precond * image)), "gz")
 
 
 def along_line(array, along_dim):

time: 229 us -> 194 us (0.85)
  blocking collectives: 83 us -> 49.7 us
  waiting for transfers between devices: 35.7 us -> 33.1 us
    psum x2 -> x4, blocking collectives: 83 us -> 49.7 us  [the longest x2 25 us: apply_weights(): row_out = lax.psum(tile_in, axis_name=a_name)]
    all_gather x1, waiting for transfers between devices: 17.5 us -> 14.9 us  [local(): slab_pressure = lax.all_gather(solution, 'size', axis=1, tiled=True)]
where the time goes in v1:
time: 194 us; the launch traced here: 193 us
  other arithmetic  50.5 us (26%)
  blocking collectives  49.7 us (26%)
  starting transfers between devices  34 us (18%)
  waiting for transfers between devices  33.1 us (17%)
  between operations  21.7 us (11%)
  local copies, waits for them, and re-layouts  4.25 us (2%)
    psum x2, blocking collectives, apply_weights(): row_out = lax.psum(tile_in, axis_name=a_name)  25 us
    psum x2, blocking collectives, apply_weights(): return lax.psum(row_out, axis_name=along_axis)  24.7 us
    ppermute x7, starting transfers between devices, extended(): lax.ppermute(tail, axis, [(i, (i + 1) % count) for i in range(ends)])  21.3 us
    ppermute x7, waiting for transfers between devices, extended(): lax.ppermute(tail, axis, [(i, (i + 1) % count) for i in range(ends)])  18 us
    all_gather x1, waiting for transfers between devices, local(): slab_pressure = lax.all_gather(solution, 'size', axis=1, tiled=True)  14.9 us
    ppermute x7, starting transfers between devices, extended(): lax.ppermute(head, axis, [((i + 1) % count, i) for i in range(ends)])  12.7 us
    reduce_sum x2, other arithmetic, paired_products(): jnp.sum(precond * image)  9.75 us
    mul x2, other arithmetic, apply_operator(): scaled = conduct * vector  9.73 us
  transfers between devices with their start and end apart: 15, of which 8 were waited for; matrix products, arithmetic and copies ran while one was open for 3% of the time, Pallas kernels for 0%

profile of v1, /device:TPU:4, one launch (start us, length us, event | category | flops | bytes accessed | tf_op | source)
XLA Modules:
  0.0 193.2 jit_solution(9540197274437170267)
XLA Ops:
  10.1 5.0 %fusion.39 = (f32[32,16,128]{2,1,0:T(8,128)S(1)}, pred[32,16,128]{2,1,0:T(8,128)(4,1)S(1)}, pred[32,16,128]{2,1,0:T(8,128)(4,1)S(1)}) fusion(f32[]{:T(128)} %bitcast.5, f32[]{:T(128)} %bitcast.4, f32[]{:T(128)} %bitcast.3, f32[32,16,128]{2,1,0:T(8,128)} %param.10, f32[]{:T(128)} %bitcast.2, f32[]{:T(128)} %bitcast.1, f32[]{:T(128)} %bitcast, ...), kind=kLoop, calls=%fused_computation.127 | loop fusion | flops 786432 | bytes 917532 | tf_op jit(solution)/shard_map/mul | solution.py:45
  16.4 4.5 %collective-permute-start = (f32[32,1,128]{2,1,0:T(1,128)S(1)}, f32[32,1,128]{2,1,0:T(1,128)S(1)}, u32[]{:S(2)}, u32[]{:S(2)}) collective-permute-start(f32[32,1,128]{2,1,0:T(1,128)S(1)} %get-tuple-element.45), channel_id=1, source_target_pairs={{0,8},{8,16},{16,24},{1,9},{9,17},{17,25},{2,10},{10,18},{18,26},{... | collective-permute-start | bytes 49160 | tf_op jit(solution)/shard_map/ppermute | solution.py:24
  24.4 2.4 %collective-permute-start.3 = (f32[1,18,128]{2,1,0:T(8,128)S(1)}, f32[1,18,128]{2,1,0:T(8,128)S(1)}, u32[]{:S(2)}, u32[]{:S(2)}) collective-permute-start(f32[1,18,128]{2,1,0:T(8,128)S(1)} %get-tuple-element.41), channel_id=1, source_target_pairs={{0,1},{1,2},{2,3},{3,4},{4,5},{5,6},{6,7},{8,9},{9,10},{10,11},{11... | collective-permute-start | bytes 27656 | tf_op jit(solution)/shard_map/ppermute | solution.py:24
  26.8 3.5 %collective-permute-done.3 = f32[1,18,128]{2,1,0:T(8,128)S(1)} collective-permute-done((f32[1,18,128]{2,1,0:T(8,128)S(1)}, f32[1,18,128]{2,1,0:T(8,128)S(1)}, u32[]{:S(2)}, u32[]{:S(2)}) %collective-permute-start.3) | collective-permute-done | bytes 9248 | tf_op jit(solution)/shard_map/ppermute | solution.py:24
  30.7 4.9 %multiply_reduce_fusion.1 = (f32[]{:T(128)}, f32[]{:T(128)}, f32[32,16,128]{2,1,0:T(8,128)S(1)}) fusion(pred[32,16,128]{2,1,0:T(8,128)(4,1)S(1)} %get-tuple-element.27, pred[32,16,128]{2,1,0:T(8,128)(4,1)S(1)} %get-tuple-element.26, f32[]{:T(128)} %bitcast.5, f32[]{:T(128)} %bitcast.4, f32[]{:T(128)} %bitcast.3, f32[32,16,128]{2,1,0:T(8,128)S(1)} %copy-done.1, ...), kind=kLoop, calls=%fused_computation.123 | loop fusion | flops 2031614 | bytes 1493024 | tf_op jit(solution)/shard_map/reduce_sum | solution.py:52
  35.6 12.5 %all-reduce.6 = (f32[]{:T(128)}, f32[]{:T(128)}) all-reduce(f32[]{:T(128)} %get-tuple-element.4, f32[]{:T(128)} %get-tuple-element.3), channel_id=1, replica_groups=mesh['size'=4,'gz'=8] {'gz'}, use_global_device_ids=true, to_apply=%region_1.2 | all-reduce | flops 2 | bytes 16 | tf_op jit(solution)/shard_map/psum | solution.py:12
  48.1 13.3 %all-reduce.8 = (f32[]{:T(128)}, f32[]{:T(128)}) all-reduce(f32[]{:T(128)} %get-tuple-element.7, f32[]{:T(128)} %get-tuple-element.8), channel_id=1, replica_groups=mesh['size'=4,'gz'=8] {'size'}, use_global_device_ids=true, to_apply=%region_2.3 | all-reduce | flops 2 | bytes 16 | tf_op jit(solution)/shard_map/psum | solution.py:13
  62.8 4.7 %fusion.38 = (f32[32,16,128]{2,1,0:T(8,128)S(1)}, f32[]{:T(128)}) fusion(pred[32,16,128]{2,1,0:T(8,128)(4,1)S(1)} %get-tuple-element.27, pred[32,16,128]{2,1,0:T(8,128)(4,1)S(1)} %get-tuple-element.26, f32[]{:T(128)} %bitcast.5, f32[]{:T(128)} %bitcast.4, f32[]{:T(128)} %bitcast.3, f32[32,16,128]{2,1,0:T(8,128)S(1)} %get-tuple-element.24, f32[]{:T(128)S(6)} %div.19, ...), kind=kLoop, calls=%fused_computation.126 | loop fusion | flops 917503 | bytes 917536 | tf_op jit(solution)/shard_map/mul | solution.py:45
  68.8 4.7 %collective-permute-start.4 = (f32[32,1,128]{2,1,0:T(1,128)S(1)}, f32[32,1,128]{2,1,0:T(1,128)S(1)}, u32[]{:S(2)}, u32[]{:S(2)}) collective-permute-start(f32[32,1,128]{2,1,0:T(1,128)S(1)} %get-tuple-element.43), channel_id=1, source_target_pairs={{0,8},{8,16},{16,24},{1,9},{9,17},{17,25},{2,10},{10,18},{18,26},{... | collective-permute-start | bytes 49160 | tf_op jit(solution)/shard_map/ppermute | solution.py:24
  76.8 2.4 %collective-permute-start.7 = (f32[1,18,128]{2,1,0:T(8,128)S(1)}, f32[1,18,128]{2,1,0:T(8,128)S(1)}, u32[]{:S(2)}, u32[]{:S(2)}) collective-permute-start(f32[1,18,128]{2,1,0:T(8,128)S(1)} %get-tuple-element.39), channel_id=1, source_target_pairs={{0,1},{1,2},{2,3},{3,4},{4,5},{5,6},{6,7},{8,9},{9,10},{10,11},{11... | collective-permute-start | bytes 27656 | tf_op jit(solution)/shard_map/ppermute | solution.py:24
  79.3 3.5 %collective-permute-done.7 = f32[1,18,128]{2,1,0:T(8,128)S(1)} collective-permute-done((f32[1,18,128]{2,1,0:T(8,128)S(1)}, f32[1,18,128]{2,1,0:T(8,128)S(1)}, u32[]{:S(2)}, u32[]{:S(2)}) %collective-permute-start.7) | collective-permute-done | bytes 9248 | tf_op jit(solution)/shard_map/ppermute | solution.py:24
  83.2 4.9 %fusion.28 = f32[]{:T(128)} fusion(f32[34,18,130]{2,1,0:T(8,128)S(1)} %select_maximum_fusion.8, f32[32,16,128]{2,1,0:T(8,128)S(1)} %get-tuple-element.37, f32[32,1,128]{2,1,0:T(1,128)S(1)} %collective-permute-done.4, f32[32,1,128]{2,1,0:T(1,128)S(1)} %collective-permute-done.5, f32[1,18,128]{2,1,0:T(8,128)S(1)} %collective-permute-done.7, ...), kind=kLoop, calls=%fused_computation.91 | loop fusion | flops 2031615 | bytes 1493024 | tf_op jit(solution)/shard_map/reduce_sum | solution.py:52
  88.1 12.5 %all-reduce.5 = (f32[]{:T(128)}, f32[]{:T(128)}) all-reduce(f32[]{:T(128)} %get-tuple-element.38, f32[]{:T(128)} %fusion.28), channel_id=1, replica_groups=mesh['size'=4,'gz'=8] {'gz'}, use_global_device_ids=true, to_apply=%region_7.8 | all-reduce | flops 2 | bytes 16 | tf_op jit(solution)/shard_map/psum | solution.py:12
  100.6 11.4 %all-reduce.7 = (f32[]{:T(128)}, f32[]{:T(128)}) all-reduce(f32[]{:T(128)} %get-tuple-element.5, f32[]{:T(128)} %get-tuple-element.6), channel_id=1, replica_groups=mesh['size'=4,'gz'=8] {'size'}, use_global_device_ids=true, to_apply=%region_8.9 | all-reduce | flops 2 | bytes 16 | tf_op jit(solution)/shard_map/psum | solution.py:13
  116.6 4.7 %multiply_add_fusion.6 = f32[32,16,128]{2,1,0:T(8,128)} fusion(f32[]{:T(128)S(6)} %div.21, f32[]{:T(128)S(6)} %div.23, f32[]{:T(128)S(6)} %div.19, pred[32,16,128]{2,1,0:T(8,128)(4,1)S(1)} %get-tuple-element.27, pred[32,16,128]{2,1,0:T(8,128)(4,1)S(1)} %get-tuple-element.26, f32[]{:T(128)} %bitcast.5, f32[]{:T(128)} %bitcast.4, f32[]{:T(128)} %bitcast.3, ...), kind=kLoop, calls=%fused_computation.120 | loop fusion | flops 1114112 | bytes 917540 | tf_op jit(solution)/shard_map/add | solution.py:125
  123.3 2.4 %collective-permute-start.10 = (f32[1,64,128]{2,1,0:T(8,128)S(1)}, f32[1,64,128]{2,1,0:T(8,128)S(1)}, u32[]{:S(2)}, u32[]{:S(2)}) collective-permute-start(f32[1,64,128]{2,1,0:T(8,128)S(1)} %get-tuple-element.35), channel_id=1, source_target_pairs={{0,1},{1,2},{2,3},{3,4},{4,5},{5,6},{6,7},{8,9},{9,10},{10,11},{11... | collective-permute-start | bytes 98312 | tf_op jit(solution)/shard_map/ppermute | solution.py:24
  127.6 2.3 %select_bitcast_fusion.1 = (f32[1,32,64,128]{3,2,1,0:T(8,128)S(1)}, pred[32,64,128]{2,1,0:T(8,128)(4,1)S(1)}, pred[32,64,128]{2,1,0:T(8,128)(4,1)S(1)}) fusion(f32[]{:T(128)} %bitcast.5, f32[]{:T(128)} %bitcast.4, f32[]{:T(128)} %bitcast.3, s32[32,64,128]{2,1,0:T(8,128)S(1)} %copy-done.3), kind=kLoop, calls=%fused_computation.70 | loop fusion | flops 1048576 | bytes 2621452 | tf_op jit(solution)/shard_map/stack | solution.py:139
  131.8 14.9 %all-gather.2.cloned.1.call-done = f32[32,64,128]{2,1,0:T(8,128)} async-done(((f32[32,16,128]{2,1,0:T(8,128)}), f32[32,64,128]{2,1,0:T(8,128)}) %all-gather.2.cloned.1.call-update) | async-done | bytes 1048592 | tf_op jit(solution)/shard_map/all_gather | solution.py:138
  147.6 2.5 %collective-permute-start.9 = (f32[3,2,64,128]{3,2,1,0:T(8,128)S(1)}, f32[3,2,64,128]{3,2,1,0:T(8,128)S(1)}, u32[]{:S(2)}, u32[]{:S(2)}) collective-permute-start(f32[3,2,64,128]{3,2,1,0:T(8,128)S(1)} %get-tuple-element.32), channel_id=1, source_target_pairs={{1,0},{2,1},{3,2},{4,3},{5,4},{6,5},{7,6},{9,8},{10,9},{11,10},{12... | collective-permute-start | bytes 589832 | tf_op jit(solution)/shard_map/ppermute | solution.py:26
  153.3 4.7 %collective-permute-done.8 = f32[3,2,64,128]{3,2,1,0:T(8,128)S(1)} collective-permute-done((f32[3,2,64,128]{3,2,1,0:T(8,128)S(1)}, f32[3,2,64,128]{3,2,1,0:T(8,128)S(1)}, u32[]{:S(2)}, u32[]{:S(2)}) %collective-permute-start.8) | collective-permute-done | bytes 196640 | tf_op jit(solution)/shard_map/ppermute | solution.py:24
  158.0 7.3 %select_maximum_fusion = f32[3,36,66,130]{3,2,1,0:T(8,128)S(1)} fusion(f32[3,2,64,128]{3,2,1,0:T(8,128)S(1)} %collective-permute-done.9, f32[3,2,64,128]{3,2,1,0:T(8,128)S(1)} %collective-permute-done.8, f32[1,32,64,128]{3,2,1,0:T(8,128)S(1)} %select_bitcast_fusion, f32[1,32,64,128]{3,2,1,0:T(8,128)S(1)} %get-tuple-element.21, f32[1,32,64,128]{3,2,1,0:T(8,128)S(1)} %bitcast.52), kind=kLoop, calls=%fused_computation.4 | loop fusion | flops 19459440 | bytes 7245504 | tf_op jit(solution)/shard_map/concatenate | solution.py:22
  165.9 2.4 %multiply_add_fusion.1 = (f32[32,64,129]{2,1,0:T(8,128)S(1)}, f32[32,64,129]{2,1,0:T(8,128)S(1)}) fusion(f32[34,66,130]{2,1,0:T(8,128)S(1)} %select_maximum_fusion.6, f32[]{:T(128)} %bitcast.45, f32[34,66,130]{2,1,0:T(8,128)S(1)} %get-tuple-element.29, f32[34,66,130]{2,1,0:T(8,128)S(1)} %get-tuple-element.28, f32[]{:T(128)} %bitcast.42), kind=kLoop, calls=%fused_computation.30 | loop fusion | flops 3170304 | bytes 8454152 | tf_op jit(solution)/shard_map/add | solution.py:82
  175.5 2.6 %collective-permute-start.12 = (f32[1,64,128]{2,1,0:T(8,128)S(1)}, f32[1,64,128]{2,1,0:T(8,128)S(1)}, u32[]{:S(2)}, u32[]{:S(2)}) collective-permute-start(f32[1,64,128]{2,1,0:T(8,128)S(1)} %get-tuple-element.33), channel_id=1, source_target_pairs={{0,1},{1,2},{2,3},{3,4},{4,5},{5,6},{6,7},{8,9},{9,10},{10,11},{11... | collective-permute-start | bytes 98312 | tf_op jit(solution)/shard_map/ppermute | solution.py:24
  178.1 3.5 %collective-permute-done.12 = f32[1,64,128]{2,1,0:T(8,128)S(1)} collective-permute-done((f32[1,64,128]{2,1,0:T(8,128)S(1)}, f32[1,64,128]{2,1,0:T(8,128)S(1)}, u32[]{:S(2)}, u32[]{:S(2)}) %collective-permute-start.12) | collective-permute-done | bytes 32800 | tf_op jit(solution)/shard_map/ppermute | solution.py:24
  (62 shorter events, 34.1 us)
Async XLA Ops:
  7.2 23.5 %copy-start.1 = (f32[32,16,128]{2,1,0:T(8,128)S(1)}, f32[32,16,128]{2,1,0:T(8,128)}, u32[]{:S(2)}) copy-start(f32[32,16,128]{2,1,0:T(8,128)} %param.10) | copy-start | bytes 786436
  7.2 139.5 %all-gather.2.cloned.1.call-start = ((), (), s32[]{:S(2)}) async-start(), calls=%async_computation | async-start | bytes 1310720 | tf_op jit(solution)/shard_map/all_gather | solution.py:138
  15.1 5.9 %collective-permute-start.1 = (f32[32,1,128]{2,1,0:T(1,128)S(1)}, f32[32,1,128]{2,1,0:T(1,128)S(1)}, u32[]{:S(2)}, u32[]{:S(2)}) collective-permute-start(f32[32,1,128]{2,1,0:T(1,128)S(1)} %get-tuple-element.46), channel_id=1, source_target_pairs={{8,0},{16,8},{24,16},{9,1},{17,9},{25,17},{10,2},{18,10},{26,18},{... | collective-permute-start | bytes 49160 | tf_op jit(solution)/shard_map/ppermute | solution.py:26
  16.4 6.0 %collective-permute-start = (f32[32,1,128]{2,1,0:T(1,128)S(1)}, f32[32,1,128]{2,1,0:T(1,128)S(1)}, u32[]{:S(2)}, u32[]{:S(2)}) collective-permute-start(f32[32,1,128]{2,1,0:T(1,128)S(1)} %get-tuple-element.45), channel_id=1, source_target_pairs={{0,8},{8,16},{16,24},{1,9},{9,17},{17,25},{2,10},{10,18},{18,26},{... | collective-permute-start | bytes 49160 | tf_op jit(solution)/shard_map/ppermute | solution.py:24
  22.4 4.3 %collective-permute-start.2 = (f32[1,18,128]{2,1,0:T(8,128)S(1)}, f32[1,18,128]{2,1,0:T(8,128)S(1)}, u32[]{:S(2)}, u32[]{:S(2)}) collective-permute-start(f32[1,18,128]{2,1,0:T(8,128)S(1)} %get-tuple-element.42), channel_id=1, source_target_pairs={{1,0},{2,1},{3,2},{4,3},{5,4},{6,5},{7,6},{9,8},{10,9},{11,10},{12... | collective-permute-start | bytes 27656 | tf_op jit(solution)/shard_map/ppermute | solution.py:26
  24.4 5.9 %collective-permute-start.3 = (f32[1,18,128]{2,1,0:T(8,128)S(1)}, f32[1,18,128]{2,1,0:T(8,128)S(1)}, u32[]{:S(2)}, u32[]{:S(2)}) collective-permute-start(f32[1,18,128]{2,1,0:T(8,128)S(1)} %get-tuple-element.41), channel_id=1, source_target_pairs={{0,1},{1,2},{2,3},{3,4},{4,5},{5,6},{6,7},{8,9},{9,10},{10,11},{11... | collective-permute-start | bytes 27656 | tf_op jit(solution)/shard_map/ppermute | solution.py:24
  67.5 6.0 %collective-permute-start.5 = (f32[32,1,128]{2,1,0:T(1,128)S(1)}, f32[32,1,128]{2,1,0:T(1,128)S(1)}, u32[]{:S(2)}, u32[]{:S(2)}) collective-permute-start(f32[32,1,128]{2,1,0:T(1,128)S(1)} %get-tuple-element.44), channel_id=1, source_target_pairs={{8,0},{16,8},{24,16},{9,1},{17,9},{25,17},{10,2},{18,10},{26,18},{... | collective-permute-start | bytes 49160 | tf_op jit(solution)/shard_map/ppermute | solution.py:26
  68.8 52.6 %copy-start = (f32[1,32,64,128]{3,2,1,0:T(8,128)S(1)}, f32[1,32,64,128]{3,2,1,0:T(8,128)}, u32[]{:S(2)}) copy-start(f32[1,32,64,128]{3,2,1,0:T(8,128)} %param.16) | copy-start | bytes 3145732
  68.8 58.2 %copy-start.9 = (f32[1,3]{1,0:T(1,128)S(1)}, f32[1,3]{1,0:T(1,128)}, u32[]{:S(2)}) copy-start(f32[1,3]{1,0:T(1,128)} %param.13) | copy-start | bytes 40
  68.8 58.8 %copy-start.3 = (s32[32,64,128]{2,1,0:T(8,128)S(1)}, s32[32,64,128]{2,1,0:T(8,128)}, u32[]{:S(2)}) copy-start(s32[32,64,128]{2,1,0:T(8,128)} %param.9) | copy-start | bytes 3145732
  68.8 6.1 %collective-permute-start.4 = (f32[32,1,128]{2,1,0:T(1,128)S(1)}, f32[32,1,128]{2,1,0:T(1,128)S(1)}, u32[]{:S(2)}, u32[]{:S(2)}) collective-permute-start(f32[32,1,128]{2,1,0:T(1,128)S(1)} %get-tuple-element.43), channel_id=1, source_target_pairs={{0,8},{8,16},{16,24},{1,9},{9,17},{17,25},{2,10},{10,18},{18,26},{... | collective-permute-start | bytes 49160 | tf_op jit(solution)/shard_map/ppermute | solution.py:24
  74.9 4.3 %collective-permute-start.6 = (f32[1,18,128]{2,1,0:T(8,128)S(1)}, f32[1,18,128]{2,1,0:T(8,128)S(1)}, u32[]{:S(2)}, u32[]{:S(2)}) collective-permute-start(f32[1,18,128]{2,1,0:T(8,128)S(1)} %get-tuple-element.40), channel_id=1, source_target_pairs={{1,0},{2,1},{3,2},{4,3},{5,4},{6,5},{7,6},{9,8},{10,9},{11,10},{12... | collective-permute-start | bytes 27656 | tf_op jit(solution)/shard_map/ppermute | solution.py:26
  76.8 5.9 %collective-permute-start.7 = (f32[1,18,128]{2,1,0:T(8,128)S(1)}, f32[1,18,128]{2,1,0:T(8,128)S(1)}, u32[]{:S(2)}, u32[]{:S(2)}) collective-permute-start(f32[1,18,128]{2,1,0:T(8,128)S(1)} %get-tuple-element.39), channel_id=1, source_target_pairs={{0,1},{1,2},{2,3},{3,4},{4,5},{5,6},{6,7},{8,9},{9,10},{10,11},{11... | collective-permute-start | bytes 27656 | tf_op jit(solution)/shard_map/ppermute | solution.py:24
  121.4 30.9 %collective-permute-start.11 = (f32[1,64,128]{2,1,0:T(8,128)S(1)}, f32[1,64,128]{2,1,0:T(8,128)S(1)}, u32[]{:S(2)}, u32[]{:S(2)}) collective-permute-start(f32[1,64,128]{2,1,0:T(8,128)S(1)} %get-tuple-element.36), channel_id=1, source_target_pairs={{1,0},{2,1},{3,2},{4,3},{5,4},{6,5},{7,6},{9,8},{10,9},{11,10},{12... | collective-permute-start | bytes 98312 | tf_op jit(solution)/shard_map/ppermute | solution.py:26
  123.3 29.0 %collective-permute-start.10 = (f32[1,64,128]{2,1,0:T(8,128)S(1)}, f32[1,64,128]{2,1,0:T(8,128)S(1)}, u32[]{:S(2)}, u32[]{:S(2)}) collective-permute-start(f32[1,64,128]{2,1,0:T(8,128)S(1)} %get-tuple-element.35), channel_id=1, source_target_pairs={{0,1},{1,2},{2,3},{3,4},{4,5},{5,6},{6,7},{8,9},{9,10},{10,11},{11... | collective-permute-start | bytes 98312 | tf_op jit(solution)/shard_map/ppermute | solution.py:24
  147.6 10.4 %copy-start.2 = (f32[32,64,128]{2,1,0:T(8,128)S(1)}, f32[32,64,128]{2,1,0:T(8,128)}, u32[]{:S(2)}) copy-start(f32[32,64,128]{2,1,0:T(8,128)} %all-gather.2.cloned.1.call-done) | copy-start | bytes 3145732
  147.6 5.6 %collective-permute-start.9 = (f32[3,2,64,128]{3,2,1,0:T(8,128)S(1)}, f32[3,2,64,128]{3,2,1,0:T(8,128)S(1)}, u32[]{:S(2)}, u32[]{:S(2)}) collective-permute-start(f32[3,2,64,128]{3,2,1,0:T(8,128)S(1)} %get-tuple-element.32), channel_id=1, source_target_pairs={{1,0},{2,1},{3,2},{4,3},{5,4},{6,5},{7,6},{9,8},{10,9},{11,10},{12... | collective-permute-start | bytes 589832 | tf_op jit(solution)/shard_map/ppermute | solution.py:26
  150.1 7.9 %collective-permute-start.8 = (f32[3,2,64,128]{3,2,1,0:T(8,128)S(1)}, f32[3,2,64,128]{3,2,1,0:T(8,128)S(1)}, u32[]{:S(2)}, u32[]{:S(2)}) collective-permute-start(f32[3,2,64,128]{3,2,1,0:T(8,128)S(1)} %get-tuple-element.31), channel_id=1, source_target_pairs={{0,1},{1,2},{2,3},{3,4},{4,5},{5,6},{6,7},{8,9},{9,10},{10,11},{11... | collective-permute-start | bytes 589832 | tf_op jit(solution)/shard_map/ppermute | solution.py:24
  152.3 5.7 %copy-start.5 = (f32[1,64,128]{2,1,0:T(8,128)}, f32[1,64,128]{2,1,0:T(8,128)S(1)}, u32[]{:S(2)}) copy-start(f32[1,64,128]{2,1,0:T(8,128)S(1)} %collective-permute-done.11) | copy-start | bytes 98308
  152.3 5.7 %copy-start.7 = (f32[1,64,128]{2,1,0:T(8,128)}, f32[1,64,128]{2,1,0:T(8,128)S(1)}, u32[]{:S(2)}) copy-start(f32[1,64,128]{2,1,0:T(8,128)S(1)} %collective-permute-done.10) | copy-start | bytes 98308
  168.3 1.9 copy-start.6
  168.3 1.9 copy-start.8
  173.6 4.6 %collective-permute-start.13 = (f32[1,64,128]{2,1,0:T(8,128)S(1)}, f32[1,64,128]{2,1,0:T(8,128)S(1)}, u32[]{:S(2)}, u32[]{:S(2)}) collective-permute-start(f32[1,64,128]{2,1,0:T(8,128)S(1)} %get-tuple-element.34), channel_id=1, source_target_pairs={{1,0},{2,1},{3,2},{4,3},{5,4},{6,5},{7,6},{9,8},{10,9},{11,10},{12... | collective-permute-start | bytes 98312 | tf_op jit(solution)/shard_map/ppermute | solution.py:26
  175.5 6.1 %collective-permute-start.12 = (f32[1,64,128]{2,1,0:T(8,128)S(1)}, f32[1,64,128]{2,1,0:T(8,128)S(1)}, u32[]{:S(2)}, u32[]{:S(2)}) collective-permute-start(f32[1,64,128]{2,1,0:T(8,128)S(1)} %get-tuple-element.33), channel_id=1, source_target_pairs={{0,1},{1,2},{2,3},{3,4},{4,5},{5,6},{6,7},{8,9},{9,10},{10,11},{11... | collective-permute-start | bytes 98312 | tf_op jit(solution)/shard_map/ppermute | solution.py:24
  (1 other events, 1.2 us)
Sparse Core Ops, SparseCore 0:
  121.5 25.2 all-gather.1
